TPU v7x, 32 devices: a whole 2x2x4 slice. The times are simulated.
32 devices in a mesh: experts: 4 (over z), context: 4 (over y, x), dp: 2 (over core).
Axes of the slice: x: 2, y: 2, z: 4, core: 2. Of those that a mesh axis runs over, the one named last changes fastest.
Arguments:
- tokens: bfloat16 [8, 4096, 512], P(('experts', 'dp'), 'context'), may hold values from -6 to 6
- attn_gain: float32 [512], replicated, may hold values from 0.5 to 1.5
- mix_gain: float32 [512], replicated, may hold values from 0.5 to 1.5
- query_key_value_weight: bfloat16 [512, 1536], replicated, may hold values from -0.375 to 0.375
- output_weight: bfloat16 [512, 512], replicated, may hold values from -0.75 to 0.75
- router_weight: bfloat16 [512, 8], replicated, may hold values from -0.1875 to 0.1875
- w_in: bfloat16 [8, 512, 2048], P('experts'), may hold values from -1.5 to 1.5
- w_exp_out: bfloat16 [8, 2048, 512], P('experts'), may hold values from -1 to 1
- out_grad: bfloat16 [8, 4096, 512], P(('experts', 'dp'), 'context'), may hold values from -6 to 6
- group_slot: int32 [8, 4096], P(('experts', 'dp'), 'context'), may hold values from 0 to 1023, as said below
- group_routes: int32 [1024, 4], P(('experts', 'context', 'dp')), may hold values from 0 to 7, all different within a row
- route_order: int32 [1024, 4], P(('experts', 'context', 'dp')), may hold values from 0 to 127, as said below
Outputs:
- layer_out: bfloat16 [8, 4096, 512], P(('experts', 'dp'), 'context')
- token_grad: float32 [8, 4096, 512], P(('experts', 'dp'), 'context')
- attn_gain_grad: float32 [512], replicated
- mix_gain_grad: float32 [512], replicated
- qkv_grad: float32 [512, 1536], replicated
- out_proj_grad: float32 [512, 512], replicated
- route_grad: float32 [512, 8], replicated
- expert_in_grad: float32 [8, 512, 2048], P('experts')
- expert_out_grad: float32 [8, 2048, 512], P('experts')
Inputs may be any that keep to these rules, and one draw needn't show every extreme that they name: `group_slot`: in each run of 1024 positions c * 1024 to c * 1024 + 1023 of a sequence, every slot appears exactly once. `group_routes`: each row names 4 different experts; every expert is named by some row. `route_order`: in each aligned block of 32 rows, all 128 entries differ.
All inputs are finite; a program needn't handle non-finite values.
Results may differ from a plain program's by a relative error of at most 0.028.
Values may be sent and summed in bfloat16 or wider, within the bound.
A program may use at most 256 MiB of HBM per device.

v0:
```python
from functools import partial
import math
import jax
import jax.numpy as jnp
from jax import lax
from jax.sharding import PartitionSpec as P

HEADS = 8
NORM_EPS = 1e-05
MASKED = -1e30


def passed_along(block, axis, distance):
    devices = range(lax.axis_size(axis))
    route = [((i - distance) % len(devices), i) for i in devices]
    return lax.ppermute(block, axis, route)


def smooth_gate(values):
    return jax.nn.gelu(values, approximate=True)


def norm_forward(values, gain):
    inv_rms = lax.rsqrt(jnp.mean(values * values, axis=-1, keepdims=True) + NORM_EPS)
    return (values * inv_rms * gain, inv_rms)


def norm_backward(values, inv_rms, gain, grad_normed):
    normed = values * inv_rms
    scaled_grad = grad_normed * gain
    gain_grad = jnp.sum(grad_normed * normed, axis=0)
    inner_mean = jnp.mean(scaled_grad * normed, axis=-1, keepdims=True)
    return (inv_rms * (scaled_grad - normed * inner_mean), gain_grad)


def place_pairs(route_flat, order_flat, capacity, experts):
    same_expert = route_flat[:, None] == route_flat[None, :]
    earlier = order_flat[None, :] < order_flat[:, None]
    ranks = jnp.sum((same_expert & earlier).astype(jnp.int32), axis=1)
    return jnp.where(ranks < capacity, route_flat * capacity + ranks, experts * capacity)


def split_heads(matrix, head_count):
    return matrix.reshape(matrix.shape[0], head_count, matrix.shape[1] // head_count)


def fold_keys(carried_in, keyval, first_key, queries, first_query, block_keys):
    half_width = keyval.shape[1] // 2
    head_count = queries.shape[1]
    query_rows = queries.shape[0]
    score_scale = queries.shape[2] ** (-0.5)
    query_pos = first_query + jnp.arange(query_rows)
    block_count = jnp.clip(
        (first_query + query_rows + block_keys - 1) // block_keys, 0, keyval.shape[0] // block_keys
    )

    def fold_visit_block(step_index, carried):
        run_peak, run_total, run_accum = carried
        kv_block = lax.dynamic_slice_in_dim(keyval, step_index * block_keys, block_keys, 0)
        key_heads = split_heads(kv_block[:, :half_width], head_count)
        value_heads = split_heads(kv_block[:, half_width:], head_count)
        scores = (
            jnp.einsum("qhd,khd->hqk", queries, key_heads, preferred_element_type=jnp.float32)
            * score_scale
        )
        key_pos = step_index * block_keys + jnp.arange(block_keys)
        allowed = key_pos[None, None, :] <= query_pos[None, :, None]
        scores = jnp.where(allowed, scores, MASKED)
        new_peak = jnp.maximum(run_peak, jnp.max(scores, axis=-1))
        weights = jnp.where(allowed, jnp.exp(scores - new_peak[:, :, None]), 0.0)
        factor = jnp.exp(run_peak - new_peak)
        run_total = run_total * factor + jnp.sum(weights, axis=-1)
        update = jnp.einsum(
            "hqk,khd->qhd",
            weights.astype(jnp.bfloat16),
            value_heads,
            preferred_element_type=jnp.float32,
        )
        run_accum = run_accum * jnp.transpose(factor)[:, :, None] + update
        return (new_peak, run_total, run_accum)

    return lax.fori_loop(0, block_count, fold_visit_block, carried_in)


def back_keys(gathered, queries, grad_heads, delta_rows, log_total, first_query, block_keys):
    half_width = gathered.shape[1] // 2
    head_count = queries.shape[1]
    query_rows = queries.shape[0]
    score_scale = queries.shape[2] ** (-0.5)
    query_pos = first_query + jnp.arange(query_rows)
    block_count = (first_query + query_rows + block_keys - 1) // block_keys

    def back_visit_block(step_index, carried):
        grad_query, grad_keyval = carried
        kv_block = lax.dynamic_slice_in_dim(gathered, step_index * block_keys, block_keys, 0)
        key_heads = split_heads(kv_block[:, :half_width], head_count)
        value_heads = split_heads(kv_block[:, half_width:], head_count)
        scores = (
            jnp.einsum("qhd,khd->hqk", queries, key_heads, preferred_element_type=jnp.float32)
            * score_scale
        )
        key_pos = step_index * block_keys + jnp.arange(block_keys)
        allowed = key_pos[None, None, :] <= query_pos[None, :, None]
        probs_full = jnp.where(allowed, jnp.exp(scores - log_total[:, :, None]), 0.0)
        grad_value = jnp.einsum(
            "hqk,qhd->khd",
            probs_full.astype(jnp.bfloat16),
            grad_heads,
            preferred_element_type=jnp.float32,
        )
        grad_probs = jnp.einsum(
            "qhd,khd->hqk", grad_heads, value_heads, preferred_element_type=jnp.float32
        )
        grad_scores = (probs_full * (grad_probs - delta_rows[:, :, None])).astype(jnp.bfloat16)
        grad_query = (
            grad_query
            + jnp.einsum("hqk,khd->qhd", grad_scores, key_heads, preferred_element_type=jnp.float32)
            * score_scale
        )
        grad_key = (
            jnp.einsum("hqk,qhd->khd", grad_scores, queries, preferred_element_type=jnp.float32)
            * score_scale
        )
        merged = jnp.concatenate(
            [grad_key.reshape(block_keys, half_width), grad_value.reshape(block_keys, half_width)],
            axis=1,
        )
        grad_keyval = lax.dynamic_update_slice_in_dim(
            grad_keyval, merged, step_index * block_keys, 0
        )
        return (grad_query, grad_keyval)

    initial = (jnp.zeros(queries.shape, jnp.float32), jnp.zeros(gathered.shape, jnp.float32))
    return lax.fori_loop(0, block_count, back_visit_block, initial)


def per_device(
    tokens,
    attn_gain,
    mix_gain,
    query_key_value_weight,
    output_weight,
    router_weight,
    w_in,
    w_exp_out,
    out_grad,
    group_slot,
    group_routes,
    route_order,
):
    query_rows = tokens.shape[1]
    model_width = tokens.shape[2]
    head_count = HEADS
    head_size = model_width // head_count
    block_keys = math.gcd(query_rows, 512)
    first_query = lax.axis_index("context") * query_rows
    inputs = tokens[0].astype(jnp.float32)
    normed_one, inv_rms_one = norm_forward(inputs, attn_gain)
    act_low = normed_one.astype(jnp.bfloat16)
    qkv_low = jnp.dot(act_low, query_key_value_weight, preferred_element_type=jnp.float32).astype(
        jnp.bfloat16
    )
    queries = split_heads(qkv_low[:, :model_width], head_count)
    keyval = qkv_low[:, model_width:]
    initial = (
        jnp.full((head_count, query_rows), MASKED, jnp.float32),
        jnp.zeros((head_count, query_rows), jnp.float32),
        jnp.zeros((query_rows, head_count, head_size), jnp.float32),
    )
    fold_local = partial(fold_keys, queries=queries, first_query=first_query, block_keys=block_keys)
    run_peak, run_total, run_accum = fold_local(
        initial, lax.all_gather(keyval, "context", axis=0, tiled=True), jnp.int32(0)
    )
    attn_heads = run_accum / jnp.transpose(run_total)[:, :, None]
    log_total = run_peak + jnp.log(run_total)
    attention_reduced = attn_heads.reshape(query_rows, model_width).astype(jnp.bfloat16)
    residual = inputs + jnp.dot(
        attention_reduced, output_weight, preferred_element_type=jnp.float32
    )
    normed_two, inv_rms_two = norm_forward(residual, mix_gain)
    mixing_input = normed_two.astype(jnp.bfloat16)
    mixing_logits = jnp.dot(mixing_input, router_weight, preferred_element_type=jnp.float32)
    slot_row = group_slot[0]
    inverse = (
        jnp.zeros((query_rows,), jnp.int32)
        .at[slot_row]
        .set(jnp.arange(query_rows, dtype=jnp.int32))
    )
    groups, top_count = group_routes.shape
    experts = router_weight.shape[1]
    members = query_rows // groups
    capacity = 5 * groups * top_count // (4 * experts)
    local_experts = w_in.shape[0]
    sources = experts // local_experts
    slot_total = experts * capacity
    grouped_in = mixing_input[inverse].reshape(groups, members, model_width)
    grouped_logit = mixing_logits[inverse].reshape(groups, members, experts)
    route_index = jnp.broadcast_to(group_routes[:, None, :], (groups, members, top_count))
    chosen = jnp.take_along_axis(grouped_logit, route_index, axis=2)
    weights = jax.nn.softmax(chosen, axis=1)
    mix_low = weights.astype(jnp.bfloat16)
    mixed_rows = jnp.einsum(
        "gtk,gtd->gkd", mix_low, grouped_in, preferred_element_type=jnp.float32
    ).astype(jnp.bfloat16)
    pair_index = place_pairs(group_routes.reshape(-1), route_order.reshape(-1), capacity, experts)
    send_rows = (
        jnp.zeros((slot_total + 1, model_width), jnp.bfloat16)
        .at[pair_index]
        .set(mixed_rows.reshape(-1, model_width))
    )
    received = lax.all_to_all(
        send_rows[:slot_total].reshape(experts, capacity, model_width),
        "experts",
        split_axis=0,
        concat_axis=0,
        tiled=True,
    )
    received = received.reshape(sources, local_experts, capacity, model_width)
    pre_act = jnp.einsum("secd,edh->sech", received, w_in, preferred_element_type=jnp.float32)
    hidden_act, gate_pull = jax.vjp(smooth_gate, pre_act)
    hidden_low = hidden_act.astype(jnp.bfloat16)
    expert_res = jnp.einsum(
        "sech,ehd->secd", hidden_low, w_exp_out, preferred_element_type=jnp.float32
    ).astype(jnp.bfloat16)
    returned = lax.all_to_all(
        expert_res.reshape(experts, capacity, model_width),
        "experts",
        split_axis=0,
        concat_axis=0,
        tiled=True,
    )
    zero_row = jnp.zeros((1, model_width), jnp.bfloat16)
    outputs = jnp.concatenate([returned.reshape(slot_total, model_width), zero_row], axis=0)[
        pair_index
    ]
    outputs = outputs.reshape(groups, top_count, model_width)
    combined = jnp.einsum(
        "gtk,gkd->gtd", mix_low, outputs, preferred_element_type=jnp.float32
    ).reshape(query_rows, model_width)
    layer_out = (residual + combined[slot_row]).astype(jnp.bfloat16)
    grad_top = out_grad[0]
    grouped_grad = grad_top[inverse].reshape(groups, members, model_width)
    grad_w_comb = jnp.einsum(
        "gtd,gkd->gtk", grouped_grad, outputs, preferred_element_type=jnp.float32
    )
    grad_out_rows = jnp.einsum(
        "gtk,gtd->gkd", mix_low, grouped_grad, preferred_element_type=jnp.float32
    ).astype(jnp.bfloat16)
    grad_send = (
        jnp.zeros((slot_total + 1, model_width), jnp.bfloat16)
        .at[pair_index]
        .set(grad_out_rows.reshape(-1, model_width))
    )
    grad_recv = lax.all_to_all(
        grad_send[:slot_total].reshape(experts, capacity, model_width),
        "experts",
        split_axis=0,
        concat_axis=0,
        tiled=True,
    )
    grad_recv = grad_recv.reshape(sources, local_experts, capacity, model_width)
    w_exp_out_grad = jnp.einsum(
        "sech,secd->ehd", hidden_low, grad_recv, preferred_element_type=jnp.float32
    )
    grad_hidden = jnp.einsum(
        "secd,ehd->sech", grad_recv, w_exp_out, preferred_element_type=jnp.float32
    )
    grad_pre = gate_pull(grad_hidden)[0].astype(jnp.bfloat16)
    w_in_grad = jnp.einsum("secd,sech->edh", received, grad_pre, preferred_element_type=jnp.float32)
    grad_owner = jnp.einsum(
        "sech,edh->secd", grad_pre, w_in, preferred_element_type=jnp.float32
    ).astype(jnp.bfloat16)
    grad_back = lax.all_to_all(
        grad_owner.reshape(experts, capacity, model_width),
        "experts",
        split_axis=0,
        concat_axis=0,
        tiled=True,
    )
    grad_mixed = jnp.concatenate([grad_back.reshape(slot_total, model_width), zero_row], axis=0)[
        pair_index
    ]
    grad_mixed = grad_mixed.reshape(groups, top_count, model_width)
    grad_w_mix = jnp.einsum(
        "gkd,gtd->gtk", grad_mixed, grouped_in, preferred_element_type=jnp.float32
    )
    grad_members = jnp.einsum(
        "gtk,gkd->gtd", mix_low, grad_mixed, preferred_element_type=jnp.float32
    )
    grad_weights = grad_w_comb + grad_w_mix
    grad_chosen = weights * (grad_weights - jnp.sum(weights * grad_weights, axis=1, keepdims=True))
    route_onehot = (group_routes[:, :, None] == jnp.arange(experts)[None, None, :]).astype(
        jnp.float32
    )
    grad_grouped = jnp.einsum(
        "gtk,gke->gte", grad_chosen, route_onehot, precision=lax.Precision.HIGHEST
    ).astype(jnp.bfloat16)
    grad_logits = grad_grouped.reshape(query_rows, experts)[slot_row]
    route_grad = jnp.einsum(
        "td,te->de", mixing_input, grad_logits, preferred_element_type=jnp.float32
    )
    grad_mix = grad_members.reshape(query_rows, model_width)[slot_row] + jnp.einsum(
        "te,de->td", grad_logits, router_weight, preferred_element_type=jnp.float32
    )
    grad_norm_two, mix_gain_grad = norm_backward(residual, inv_rms_two, mix_gain, grad_mix)
    grad_residual = grad_top.astype(jnp.float32) + grad_norm_two
    grad_proj = grad_residual.astype(jnp.bfloat16)
    out_proj_grad = jnp.einsum(
        "td,te->de", attention_reduced, grad_proj, preferred_element_type=jnp.float32
    )
    grad_att = jnp.einsum(
        "te,de->td", grad_proj, output_weight, preferred_element_type=jnp.float32
    ).astype(jnp.bfloat16)
    grad_heads = split_heads(grad_att, head_count)
    delta_rows = jnp.transpose(jnp.sum(grad_heads.astype(jnp.float32) * attn_heads, axis=-1))
    keys_back = lax.all_gather(keyval, "context", axis=0, tiled=True)
    grad_query, grad_keyval = back_keys(
        keys_back, queries, grad_heads, delta_rows, log_total, first_query, block_keys
    )
    cycle_size = lax.axis_size("context")
    own_index = lax.axis_index("context")

    def take_block(block_id):
        return lax.dynamic_slice_in_dim(grad_keyval, block_id * query_rows, query_rows, 0)

    def pass_on(step_index, carried):
        moved = passed_along(carried.astype(jnp.bfloat16), "context", 1).astype(carried.dtype)
        block_id = (own_index - 2 - step_index + 2 * cycle_size) % cycle_size
        return moved + take_block(block_id)

    start_block = take_block((own_index - 1 + cycle_size) % cycle_size)
    own_keyval = lax.fori_loop(0, cycle_size - 1, pass_on, start_block)
    grad_qkv = jnp.concatenate(
        [grad_query.reshape(query_rows, model_width), own_keyval], axis=1
    ).astype(jnp.bfloat16)
    qkv_grad = jnp.einsum("td,te->de", act_low, grad_qkv, preferred_element_type=jnp.float32)
    grad_act = jnp.einsum(
        "te,de->td", grad_qkv, query_key_value_weight, preferred_element_type=jnp.float32
    )
    grad_norm_one, attn_gain_grad = norm_backward(inputs, inv_rms_one, attn_gain, grad_act)
    token_grad = grad_residual + grad_norm_one
    dense_sums = lax.psum(
        (attn_gain_grad, mix_gain_grad, qkv_grad, out_proj_grad, route_grad),
        ("experts", "context", "dp"),
    )
    expert_sums = (
        lax.psum(w_in_grad.astype(jnp.bfloat16), ("context", "dp")).astype(jnp.float32),
        lax.psum(w_exp_out_grad.astype(jnp.bfloat16), ("context", "dp")).astype(jnp.float32),
    )
    return (
        layer_out[None],
        token_grad[None],
        dense_sums[0],
        dense_sums[1],
        dense_sums[2],
        dense_sums[3],
        dense_sums[4],
        expert_sums[0],
        expert_sums[1],
    )


def solution(mesh):
    return jax.shard_map(
        per_device,
        mesh=mesh,
        in_specs=(
            P(("experts", "dp"), "context", None),
            P(),
            P(),
            P(),
            P(),
            P(),
            P("experts", None, None),
            P("experts", None, None),
            P(("experts", "dp"), "context", None),
            P(("experts", "dp"), "context"),
            P(("experts", "context", "dp"), None),
            P(("experts", "context", "dp"), None),
        ),
        out_specs=(
            P(("experts", "dp"), "context", None),
            P(("experts", "dp"), "context", None),
            P(),
            P(),
            P(),
            P(),
            P(),
            P("experts", None, None),
            P("experts", None, None),
        ),
        check_vma=False,
    )
```

profile of v0, /device:TPU:0, one launch (start us, length us, event | category | flops | bytes accessed | tf_op | source)
XLA Modules:
  0.0 1068.3 jit_solution(3388636967692149106)
XLA Ops:
  23.1 4.3 scatter_custom_fusion
  27.5 6.7 gather_fusion.4
  35.6 69.2 %all-gather.2.cloned.1.call-done = bf16[4096,1024]{1,0:T(8,128)(2,1)} async-done(((bf16[1024,1024]{1,0:T(8,128)(2,1)}), bf16[4096,1024]{1,0:T(8,128)(2,1)}) %all-gather.2.cloned.1.call-update) | async-done | bytes 8388624 | tf_op jit(solution)/shard_map/all_gather | solution.py:172
  104.8 11.9 %copy.195 = bf16[4096,1024]{0,1:T(8,128)(2,1)} copy(bf16[4096,1024]{1,0:T(8,128)(2,1)} %all-gather.2.cloned.1.call-done) | data formatting | bytes 16777216
  118.3 33.6 %while.44 = (s32[]{:T(128)}, f32[8,1024]{1,0:T(8,128)S(1)}, f32[8,1024]{1,0:T(8,128)S(1)}, f32[1024,8,64]{0,2,1:T(8,128)}, s32[]{:T(128)}, /*index=5*/bf16[4096,...) while((s32[]{:T(128)}, f32[8,1024]{1,0:T(8,128)S(1)}, ...), condition=%wide.region_4.5_spmd.clone, body=%wide.region_1.4_spmd.clone.sunk | while | flops 1129866752 | bytes 78131464 | solution.py:82
  127.7 6.0 bitcast_add_fusion.5
  144.5 6.0 bitcast_add_fusion.5
  163.7 34.4 %gather_fusion.8 = f32[4096]{0:T(1024)S(1)} fusion(f32[32,32,8]{2,1,0:T(8,128)S(1)} %bitcast.226, s32[4096]{0:T(1024)S(1)} %reshape.372), kind=kCustom, calls=%fused_computation.8 | custom fusion | bytes 81920 | tf_op jit(solution)/shard_map/jit(take_along_axis)/gather | solution.py:199
  199.3 5.1 gather_fusion.1
  209.2 4.6 all-to-all-start
  216.7 4.7 all-to-all-done
  230.9 4.3 fusion.58
  241.6 4.2 all-to-all-start.1
  246.1 4.4 bitcast_convert_fusion.1
  264.8 6.9 gather_fusion.6
  279.1 4.9 multiply_reduce_fusion
  284.0 6.9 gather_fusion.3
  293.9 4.6 multiply_add_fusion.1
  301.9 7.9 broadcast_in_dim.113
  309.7 85.8 %while.45 = (s32[]{:T(128)}, f32[1024,8,64]{0,2,1:T(8,128)}, f32[4096,1024]{0,1:T(8,128)}, s32[]{:T(128)}, bf16[4096,1024]{0,1:T(8,128)(2,1)}, /*index=5*/bf16[1...) while((s32[]{:T(128)}, f32[1024,8,64]{0,2,1:T(8,128)}, ...), condition=%wide.region_16.17_spmd.clone, body=%wide.region_15.16_spmd.clone.sunk | while | flops 2728658432 | bytes 154251664 | solution.py:134
  311.4 8.1 fusion.196
  320.0 9.3 fusion.197
  334.0 10.3 fusion.198
  344.3 6.1 convolution_multiply_fusion.2
  353.3 8.8 fusion.196
  362.5 9.5 fusion.197
  376.7 11.0 %fusion.198 = f32[8,512,64]{1,2,0:T(8,128)} fusion(bf16[1024,8,64]{0,2,1:T(8,128)(2,1)} %get-tuple-element.733, f32[8,512,1024]{2,1,0:T(8,128)} %fusion.196, f32[8,1024]{1,0:T(8,128)S(1)} %get-tuple-element.732, pred[1024,512]{0,1:T(8,128)(4,1)S(1)} %broadcast_compare_fusion.6), kind=kOutput, calls=%fused_computation.38.clone.1 | convolution fusion | flops 553648128 | bytes 19431424 | tf_op jit(solution)/shard_map/while/body/hqk,qhd->khd/dot_general | solution.py:105
  387.7 6.2 convolution_multiply_fusion.2
  399.4 4.1 copy.223
  412.0 498.4 %while.43 = (s32[]{:T(128)}, bf16[1024,1024]{1,0:T(8,128)(2,1)}, s32[]{:T(128)}, f32[4096,1024]{0,1:T(8,128)}, s32[]{:T(128)}, /*index=5*/s32[]{:T(128)}, s32[]{...) while((s32[]{:T(128)}, bf16[1024,1024]{1,0:T(8,128)(2,1)}, s32[]{:T(128)}, ...), condition=%wide.region_18.19_spmd, body=%wide.region_17.18_spmd.sunk | while | flops 3145747 | bytes 33554764 | solution.py:332
  412.0 120.4 %collective-permute-start = (bf16[1024,1024]{1,0:T(8,128)(2,1)}, bf16[1024,1024]{1,0:T(8,128)(2,1)}, u32[]{:S(2)}, u32[]{:S(2)}) collective-permute-start(bf16[1024,1024]{1,0:T(8,128)(2,1)} %get-tuple-element.753), channel_id=1, source_target_pairs={{6,0},{0,2},{2,4},{4,6},{7,1},{1,3},{3,5},{5,7},{14,8},{8,10},{10,... | collective-permute-start | bytes 6291464 | tf_op jit(solution)/shard_map/while/body/eval_jaxpr/ppermute | solution.py:16
  532.3 4.8 constant_dynamic-slice_fusion.5
  537.1 5.3 copy.266
  542.5 265.3 %collective-permute-done = bf16[1024,1024]{1,0:T(8,128)(2,1)} collective-permute-done((bf16[1024,1024]{1,0:T(8,128)(2,1)}, bf16[1024,1024]{1,0:T(8,128)(2,1)}, u32[]{:S(2)}, u32[]{:S(2)}) %collective-permute-start) | collective-permute-done | bytes 2097184 | tf_op jit(solution)/shard_map/while/body/eval_jaxpr/ppermute | solution.py:16
  807.8 5.0 convert_add_fusion.3
  812.7 4.8 constant_dynamic-slice_fusion.5
  817.5 5.3 copy.266
  822.9 34.2 %collective-permute-done = bf16[1024,1024]{1,0:T(8,128)(2,1)} collective-permute-done((bf16[1024,1024]{1,0:T(8,128)(2,1)}, bf16[1024,1024]{1,0:T(8,128)(2,1)}, u32[]{:S(2)}, u32[]{:S(2)}) %collective-permute-start) | collective-permute-done | bytes 2097184 | tf_op jit(solution)/shard_map/while/body/eval_jaxpr/ppermute | solution.py:16
  857.0 5.0 convert_add_fusion.3
  862.0 4.8 constant_dynamic-slice_fusion.5
  866.8 5.3 copy.266
  872.1 33.2 %collective-permute-done = bf16[1024,1024]{1,0:T(8,128)(2,1)} collective-permute-done((bf16[1024,1024]{1,0:T(8,128)(2,1)}, bf16[1024,1024]{1,0:T(8,128)(2,1)}, u32[]{:S(2)}, u32[]{:S(2)}) %collective-permute-start) | collective-permute-done | bytes 2097184 | tf_op jit(solution)/shard_map/while/body/eval_jaxpr/ppermute | solution.py:16
  905.4 5.0 convert_add_fusion.3
  910.4 5.4 fusion.50
  927.4 40.2 %all-reduce.2 = (f32[512]{0:T(512)}, f32[512]{0:T(512)}, f32[512,8]{0,1:T(8,128)}) all-reduce(f32[512]{0:T(512)S(1)} %get-tuple-element.429, f32[512]{0:T(512)S(1)} %copy-done.56, f32[512,8]{0,1:T(8,128)S(1)} %fusion.116), channel_id=1, replica_groups=mesh['experts'=4,'context'=4,'dp'=2] {'experts','context','dp'}, use_global_device_ids=true, to_apply=%region_21.22 | all-reduce | flops 5120 | bytes 40960 | tf_op jit(solution)/shard_map/psum | solution.py:342
  967.5 6.8 convert_element_type.136
  974.3 4.6 convert_element_type.138
  978.9 77.8 %all-reduce.8.cloned.1.call-done = (f32[512,1536]{1,0:T(8,128)}, f32[512,512]{1,0:T(8,128)}) async-done(((f32[512,1536]{1,0:T(8,128)}, f32[512,512]{1,0:T(8,128)}), (f32[512,1536]{1,0:T(8,128)}, f32[512,512]{1,0:T(8,128)})) %all-reduce.8.cloned.1.call-update) | async-done | bytes 4194320 | tf_op jit(solution)/shard_map/psum | solution.py:342
  (277 shorter events, 148.9 us)
Async XLA Ops:
  7.2 97.6 %all-gather.2.cloned.1.call-start = ((), (), s32[]{:S(2)}) async-start(), calls=%async_computation.4 | async-start | bytes 10485760 | tf_op jit(solution)/shard_map/all_gather | solution.py:172
  14.4 3.8 copy-start.50
  16.7 3.9 copy-start.61
  18.2 5.0 copy-start.58
  18.3 16.0 %copy-start.43 = (s32[32,4]{1,0:T(8,128)}, s32[32,4]{1,0:T(8,128)S(1)}, u32[]{:S(2)}) copy-start(s32[32,4]{1,0:T(8,128)S(1)} %copy.198) | copy-start | bytes 1540
  27.5 133.4 %copy-start.45 = (s32[1024]{0:T(1024)}, s32[1024]{0:T(1024)S(1)}, u32[]{:S(2)}) copy-start(s32[1024]{0:T(1024)S(1)} %fusion.96) | copy-start | bytes 12292
  34.4 82.3 %copy-start.62 = (s32[128]{0:T(128)}, s32[128]{0:T(128)S(1)}, u32[]{:S(2)}) copy-start(s32[128]{0:T(128)S(1)} %fusion.101) | copy-start | bytes 1540
  123.6 4.1 copy-start.11
  140.4 4.1 copy-start.11
  163.7 35.2 %copy-start.46 = (s32[1024]{0:T(1024)S(1)}, s32[1024]{0:T(1024)}, u32[]{:S(2)}) copy-start(s32[1024]{0:T(1024)} %copy-done.45) | copy-start | bytes 12292
  199.3 5.1 copy-start.44
  199.3 5.1 copy-start.55
  199.3 5.1 copy-start.57
  204.3 9.5 copy-start.20
  207.2 8.8 copy-start.26
  207.2 8.8 copy-start.32
  209.2 12.1 %all-to-all-start = ((bf16[8,20,512]{2,1,0:T(8,128)(2,1)}), bf16[8,20,512]{2,1,0:T(8,128)(2,1)S(1)}, u32[]{:S(2)}, u32[]{:S(2)}) async-start(bf16[8,20,512]{2,1,0:T(8,128)(2,1)} %reshape.290), calls=%async_computation | async-start | bytes 393216 | tf_op jit(solution)/shard_map/all_to_all | solution.py:211
  221.3 9.6 all-to-all-start.2
  224.7 4.3 copy-start.63
  230.9 4.3 copy-start.24
  241.6 10.5 all-to-all-start.1
  245.9 721.7 %all-reduce.10.cloned.1.call-start = ((), (), s32[]{:S(2)}) async-start(), calls=%async_computation.6 | async-start | bytes 16777216 | tf_op jit(solution)/shard_map/psum | solution.py:347
  252.1 9.8 all-to-all-start.3
  255.7 801.1 %all-reduce.8.cloned.1.call-start = ((), (), s32[]{:S(2)}) async-start(), calls=%async_computation.5 | async-start | bytes 8388608 | tf_op jit(solution)/shard_map/psum | solution.py:342
  275.1 3.9 copy-start.41
  275.1 3.9 copy-start.48
  275.1 3.9 copy-start.52
  279.1 4.9 copy-start.33
  293.9 4.6 copy-start.13
  293.9 4.6 copy-start.36
  301.9 7.9 copy-start.3
  301.9 7.9 copy-start.49
  311.4 8.5 copy-start.38
  320.0 9.3 copy-start.4
  344.3 6.1 copy-start.10
  353.3 9.2 copy-start.38
  362.5 9.5 copy-start.4
  387.7 6.2 copy-start.10
  403.5 5.1 copy-start.22
  411.9 498.4 %copy-start.17 = (bf16[1,1024,512]{1,2,0:T(8,128)(2,1)S(1)}, bf16[1,1024,512]{1,2,0:T(8,128)(2,1)}, u32[]{:S(2)}) copy-start(bf16[1,1024,512]{1,2,0:T(8,128)(2,1)} %copy-done.15) | copy-start | bytes 3145732
  411.9 498.4 %copy-start.54 = (f32[1024]{0:T(1024)S(1)}, f32[1024]{0:T(1024)}, u32[]{:S(2)}) copy-start(f32[1024]{0:T(1024)} %copy-done.53) | copy-start | bytes 12292
  411.9 498.4 %copy-start.60 = (f32[512]{0:T(512)S(1)}, f32[512]{0:T(512)}, u32[]{:S(2)}) copy-start(f32[512]{0:T(512)} %param.19) | copy-start | bytes 6148
  412.0 395.8 %collective-permute-start = (bf16[1024,1024]{1,0:T(8,128)(2,1)}, bf16[1024,1024]{1,0:T(8,128)(2,1)}, u32[]{:S(2)}, u32[]{:S(2)}) collective-permute-start(bf16[1024,1024]{1,0:T(8,128)(2,1)} %get-tuple-element.753), channel_id=1, source_target_pairs={{6,0},{0,2},{2,4},{4,6},{7,1},{1,3},{3,5},{5,7},{14,8},{8,10},{10,... | collective-permute-start | bytes 6291464 | tf_op jit(solution)/shard_map/while/body/eval_jaxpr/ppermute | solution.py:16
  812.7 44.3 %collective-permute-start = (bf16[1024,1024]{1,0:T(8,128)(2,1)}, bf16[1024,1024]{1,0:T(8,128)(2,1)}, u32[]{:S(2)}, u32[]{:S(2)}) collective-permute-start(bf16[1024,1024]{1,0:T(8,128)(2,1)} %get-tuple-element.753), channel_id=1, source_target_pairs={{6,0},{0,2},{2,4},{4,6},{7,1},{1,3},{3,5},{5,7},{14,8},{8,10},{10,... | collective-permute-start | bytes 6291464 | tf_op jit(solution)/shard_map/while/body/eval_jaxpr/ppermute | solution.py:16
  862.0 43.4 %collective-permute-start = (bf16[1024,1024]{1,0:T(8,128)(2,1)}, bf16[1024,1024]{1,0:T(8,128)(2,1)}, u32[]{:S(2)}, u32[]{:S(2)}) collective-permute-start(bf16[1024,1024]{1,0:T(8,128)(2,1)} %get-tuple-element.753), channel_id=1, source_target_pairs={{6,0},{0,2},{2,4},{4,6},{7,1},{1,3},{3,5},{5,7},{14,8},{8,10},{10,... | collective-permute-start | bytes 6291464 | tf_op jit(solution)/shard_map/while/body/eval_jaxpr/ppermute | solution.py:16
  918.0 4.1 copy-start.8
  967.5 6.8 copy-start.27
  1056.8 3.8 copy-start.37
  (33 other events, 75.0 us)
Sparse Core Ops, SparseCore 0:
  14.5 90.2 all-gather.1
  250.7 227.8 all-reduce.9
  915.9 140.8 all-reduce.7
where the time goes:
time: 1080 us; the launch traced here: 1070 us
  waiting for transfers between devices  490 us (45%)
  local copies, waits for them, and re-layouts  192 us (18%)
  matrix products  139 us (13%)
  starting transfers between devices  136 us (13%)
  other arithmetic  54.6 us (5%)
  blocking collectives  40.2 us (4%)
  between operations  14.6 us (1%)
    ppermute x3, waiting for transfers between devices, passed_along(): return lax.ppermute(block, axis, route)  333 us
    ppermute x3, starting transfers between devices, passed_along(): return lax.ppermute(block, axis, route)  120 us
    psum x1, waiting for transfers between devices, per_device(): lax.psum((attn_gain_grad, mix_gain_grad, qkv_grad, out_proj_grad, route_g...  77.8 us
    all_gather x1, waiting for transfers between devices, per_device(): lax.all_gather(keyval, 'context', axis=0, tiled=True)  69.2 us
    psum x1, blocking collectives, per_device(): lax.psum((attn_gain_grad, mix_gain_grad, qkv_grad, out_proj_grad, route_g...  40.2 us
    gather x5, local copies, waits for them, and re-layouts, per_device(): chosen = jnp.take_along_axis(grouped_logit, route_index, axis=2)  35.7 us
    dynamic_slice x7, local copies, waits for them, and re-layouts, take_block(): lax.dynamic_slice_in_dim(grad_keyval, block_id * query_rows, query_rows, 0)  34.2 us
    unnamed x123, local copies, waits for them, and re-layouts  31.9 us
  transfers between devices with their start and end apart: 10, of which 9 were waited for; matrix products, arithmetic and copies ran while one was open for 24% of the time, Pallas kernels for 0%

commit v1 on v0

--- a/solution.py
+++ b/solution.py
@@ -340,8 +340,10 @@
     grad_norm_one, attn_gain_grad = norm_backward(inputs, inv_rms_one, attn_gain, grad_act)
     token_grad = grad_residual + grad_norm_one
     dense_sums = lax.psum(
-        (attn_gain_grad, mix_gain_grad, qkv_grad, out_proj_grad, route_grad),
-        ("experts", "context", "dp"),
+        lax.psum(
+            (attn_gain_grad, mix_gain_grad, qkv_grad, out_proj_grad, route_grad), ("context", "dp")
+        ),
+        "experts",
     )
     expert_sums = (
         lax.psum(w_in_grad.astype(jnp.bfloat16), ("context", "dp")).astype(jnp.float32),

time: 1080 us -> 1300 us (1.20)
  waiting for transfers between devices: 490 us -> 706 us
    psum x0 -> x1, waiting for transfers between devices: none -> 146 us  [per_device(): lax.psum(lax.psum((attn_gain_grad, mix_gain_grad, qkv_grad, out_proj_grad...]
    psum x1, waiting for transfers between devices: 0.01 us -> 77.2 us  [per_device(): lax.psum(w_in_grad.astype(jnp.bfloat16), ('context', 'dp'))]
    psum x0 -> x1, blocking collectives: none -> 19.6 us  [per_device(): lax.psum(lax.psum((attn_gain_grad, mix_gain_grad, qkv_grad, out_proj_grad...]
    psum x1, blocking collectives: 40.2 us -> 24.6 us  [per_device(): lax.psum((attn_gain_grad, mix_gain_grad, qkv_grad, out_proj_grad, route_g...]
    unnamed x123 -> x127, local copies, waits for them, and re-layouts: 31.9 us -> 33.1 us
  transfers between devices with their start and end apart: 10 -> 11, of which waited for: 9 -> 11; matrix products, arithmetic and copies ran while one was open for 24% -> 8% of each run, Pallas kernels for 0% -> 0%
where the time goes in v1:
time: 1300 us; the launch traced here: 1290 us
  waiting for transfers between devices  706 us (54%)
  local copies, waits for them, and re-layouts  192 us (15%)
  matrix products  140 us (11%)
  starting transfers between devices  135 us (10%)
  other arithmetic  53.4 us (4%)
  blocking collectives  44.1 us (3%)
  between operations  14.7 us (1%)
    ppermute x3, waiting for transfers between devices, passed_along(): return lax.ppermute(block, axis, route)  334 us
    psum x1, waiting for transfers between devices, per_device(): lax.psum(lax.psum((attn_gain_grad, mix_gain_grad, qkv_grad, out_proj_grad...  146 us
    ppermute x3, starting transfers between devices, passed_along(): return lax.ppermute(block, axis, route)  119 us
    psum x1, waiting for transfers between devices, per_device(): lax.psum(w_in_grad.astype(jnp.bfloat16), ('context', 'dp'))  77.2 us
    psum x1, waiting for transfers between devices, per_device(): lax.psum((attn_gain_grad, mix_gain_grad, qkv_grad, out_proj_grad, route_g...  70.2 us
    all_gather x1, waiting for transfers between devices, per_device(): lax.all_gather(keyval, 'context', axis=0, tiled=True)  69.2 us
    gather x5, local copies, waits for them, and re-layouts, per_device(): chosen = jnp.take_along_axis(grouped_logit, route_index, axis=2)  35.7 us
    dynamic_slice x7, local copies, waits for them, and re-layouts, take_block(): lax.dynamic_slice_in_dim(grad_keyval, block_id * query_rows, query_rows, 0)  34.2 us
  transfers between devices with their start and end apart: 11, of which 11 were waited for; matrix products, arithmetic and copies ran while one was open for 8% of the time, Pallas kernels for 0%

profile of v1, /device:TPU:0, one launch (start us, length us, event | category | flops | bytes accessed | tf_op | source)
XLA Modules:
  0.0 1286.2 jit_solution(9810823839906367686)
XLA Ops:
  27.5 6.7 gather_fusion.4
  35.6 69.2 %all-gather.2.cloned.1.call-done = bf16[4096,1024]{1,0:T(8,128)(2,1)} async-done(((bf16[1024,1024]{1,0:T(8,128)(2,1)}), bf16[4096,1024]{1,0:T(8,128)(2,1)}) %all-gather.2.cloned.1.call-update) | async-done | bytes 8388624 | tf_op jit(solution)/shard_map/all_gather | solution.py:172
  104.8 11.9 copy.195
  118.3 33.6 %while.44 = (s32[]{:T(128)}, f32[8,1024]{1,0:T(8,128)S(1)}, f32[8,1024]{1,0:T(8,128)S(1)}, f32[1024,8,64]{0,2,1:T(8,128)}, s32[]{:T(128)}, /*index=5*/bf16[4096,...) while((s32[]{:T(128)}, f32[8,1024]{1,0:T(8,128)S(1)}, ...), condition=%wide.region_4.5_spmd.clone, body=%wide.region_1.4_spmd.clone.sunk | while | flops 1129866752 | bytes 78131464 | solution.py:82
  127.7 6.0 bitcast_add_fusion.5
  144.5 6.0 bitcast_add_fusion.5
  163.7 34.4 %gather_fusion.8 = f32[4096]{0:T(1024)S(1)} fusion(f32[32,32,8]{2,1,0:T(8,128)S(1)} %bitcast.226, s32[4096]{0:T(1024)S(1)} %reshape.372), kind=kCustom, calls=%fused_computation.8 | custom fusion | bytes 81920 | tf_op jit(solution)/shard_map/jit(take_along_axis)/gather | solution.py:199
  199.3 5.1 gather_fusion.1
  209.3 4.6 all-to-all-start
  216.7 4.6 all-to-all-done
  231.0 5.2 fusion.58
  259.9 6.9 gather_fusion.6
  274.2 4.9 multiply_reduce_fusion
  279.1 6.9 gather_fusion.3
  289.0 4.6 multiply_add_fusion.1
  299.0 7.9 broadcast_in_dim.113
  306.8 84.2 %while.45 = (s32[]{:T(128)}, f32[1024,8,64]{0,2,1:T(8,128)}, f32[4096,1024]{0,1:T(8,128)}, s32[]{:T(128)}, bf16[4096,1024]{0,1:T(8,128)(2,1)}, /*index=5*/bf16[1...) while((s32[]{:T(128)}, f32[1024,8,64]{0,2,1:T(8,128)}, ...), condition=%wide.region_16.17_spmd.clone, body=%wide.region_15.16_spmd.clone.sunk | while | flops 2728658432 | bytes 154251664 | solution.py:134
  308.5 8.1 fusion.196
  317.1 9.3 fusion.197
  331.1 10.3 fusion.198
  341.4 6.1 convolution_multiply_fusion.2
  350.3 8.1 fusion.196
  358.9 9.3 fusion.197
  372.9 10.3 fusion.198
  383.2 6.1 convolution_multiply_fusion.2
  401.9 497.4 %while.43 = (s32[]{:T(128)}, bf16[1024,1024]{1,0:T(8,128)(2,1)}, s32[]{:T(128)}, f32[4096,1024]{0,1:T(8,128)}, s32[]{:T(128)}, /*index=5*/s32[]{:T(128)}, s32[]{...) while((s32[]{:T(128)}, bf16[1024,1024]{1,0:T(8,128)(2,1)}, s32[]{:T(128)}, ...), condition=%wide.region_18.19_spmd, body=%wide.region_17.18_spmd.sunk | while | flops 3145747 | bytes 33554764 | solution.py:332
  401.9 118.6 %collective-permute-start = (bf16[1024,1024]{1,0:T(8,128)(2,1)}, bf16[1024,1024]{1,0:T(8,128)(2,1)}, u32[]{:S(2)}, u32[]{:S(2)}) collective-permute-start(bf16[1024,1024]{1,0:T(8,128)(2,1)} %get-tuple-element.758), channel_id=1, source_target_pairs={{6,0},{0,2},{2,4},{4,6},{7,1},{1,3},{3,5},{5,7},{14,8},{8,10},{10,... | collective-permute-start | bytes 6291464 | tf_op jit(solution)/shard_map/while/body/eval_jaxpr/ppermute | solution.py:16
  520.5 4.8 constant_dynamic-slice_fusion.5
  525.3 5.3 copy.266
  530.6 266.4 %collective-permute-done = bf16[1024,1024]{1,0:T(8,128)(2,1)} collective-permute-done((bf16[1024,1024]{1,0:T(8,128)(2,1)}, bf16[1024,1024]{1,0:T(8,128)(2,1)}, u32[]{:S(2)}, u32[]{:S(2)}) %collective-permute-start) | collective-permute-done | bytes 2097184 | tf_op jit(solution)/shard_map/while/body/eval_jaxpr/ppermute | solution.py:16
  797.1 5.0 convert_add_fusion.3
  802.0 4.8 constant_dynamic-slice_fusion.5
  806.8 5.3 copy.266
  812.2 34.0 %collective-permute-done = bf16[1024,1024]{1,0:T(8,128)(2,1)} collective-permute-done((bf16[1024,1024]{1,0:T(8,128)(2,1)}, bf16[1024,1024]{1,0:T(8,128)(2,1)}, u32[]{:S(2)}, u32[]{:S(2)}) %collective-permute-start) | collective-permute-done | bytes 2097184 | tf_op jit(solution)/shard_map/while/body/eval_jaxpr/ppermute | solution.py:16
  846.2 5.0 convert_add_fusion.3
  851.1 4.8 constant_dynamic-slice_fusion.5
  855.9 5.3 copy.266
  861.3 33.1 %collective-permute-done = bf16[1024,1024]{1,0:T(8,128)(2,1)} collective-permute-done((bf16[1024,1024]{1,0:T(8,128)(2,1)}, bf16[1024,1024]{1,0:T(8,128)(2,1)}, u32[]{:S(2)}, u32[]{:S(2)}) %collective-permute-start) | collective-permute-done | bytes 2097184 | tf_op jit(solution)/shard_map/while/body/eval_jaxpr/ppermute | solution.py:16
  894.3 5.0 convert_add_fusion.3
  899.3 5.4 fusion.50
  905.6 4.6 bitcast_convert_fusion.1
  913.8 70.2 %all-reduce.11.cloned.1.call-done = (f32[512,1536]{1,0:T(8,128)}, f32[512,512]{1,0:T(8,128)}) async-done(((f32[512,1536]{1,0:T(8,128)}, f32[512,512]{1,0:T(8,128)}), (f32[512,1536]{1,0:T(8,128)}, f32[512,512]{1,0:T(8,128)})) %all-reduce.11.cloned.1.call-update) | async-done | bytes 4194320 | tf_op jit(solution)/shard_map/psum | solution.py:343
  995.5 24.6 %all-reduce.2 = (f32[512]{0:T(512)S(1)}, f32[512]{0:T(512)S(1)}, f32[512,8]{0,1:T(8,128)S(1)}) all-reduce(f32[512]{0:T(512)S(1)} %get-tuple-element.429, f32[512]{0:T(512)S(1)} %copy-done.58, f32[512,8]{0,1:T(8,128)S(1)} %fusion.116), channel_id=1, replica_groups=mesh['experts'=4,'context'=4,'dp'=2] {'context','dp'}, use_global_device_ids=true, to_apply=%region_21.22 | all-reduce | flops 5120 | bytes 40960 | tf_op jit(solution)/shard_map/psum | solution.py:343
  1020.1 19.6 %all-reduce.4 = (f32[512]{0:T(512)}, f32[512]{0:T(512)}, f32[512,8]{0,1:T(8,128)}) all-reduce(f32[512]{0:T(512)S(1)} %get-tuple-element.475, f32[512]{0:T(512)S(1)} %get-tuple-element.476, f32[512,8]{0,1:T(8,128)S(1)} %get-tuple-element.477), channel_id=1, replica_groups=mesh['experts'=4,'context'=4,'dp'=2] {'experts'}, use_global_device_ids=true, to_apply=%region_22.23 | all-reduce | flops 5120 | bytes 40960 | tf_op jit(solution)/shard_map/psum | solution.py:342
  1039.7 77.2 %all-reduce.15.cloned.1.call-done = (bf16[2,512,2048]{2,1,0:T(8,128)(2,1)}, bf16[2,2048,512]{2,1,0:T(8,128)(2,1)}) async-done(((bf16[2,512,2048]{2,1,0:T(8,128)(2,1)}, bf16[2,2048,512]{2,1,0:T(8,128)(2,1)}), (bf16[2,512,2048]{2,1,0:T(8,128)(2,1)}, bf16[2,2048,512]{2,1,0:T(8,128)(2,1)})) %all-reduce.15.cloned.1.call-update) | async-done | bytes 8388624 | tf_op jit(solution)/shard_map/psum | solution.py:349
  1116.9 6.8 convert_element_type.136
  1123.7 4.6 convert_element_type.138
  1128.3 146.4 %all-reduce.13.cloned.1.call-done = (f32[512,1536]{1,0:T(8,128)}, f32[512,512]{1,0:T(8,128)}) async-done(((f32[512,1536]{1,0:T(8,128)}, f32[512,512]{1,0:T(8,128)}), (f32[512,1536]{1,0:T(8,128)}, f32[512,512]{1,0:T(8,128)})) %all-reduce.13.cloned.1.call-update) | async-done | bytes 4194320 | tf_op jit(solution)/shard_map/psum | solution.py:342
  (285 shorter events, 161.2 us)
Async XLA Ops:
  7.2 97.6 %all-gather.2.cloned.1.call-start = ((), (), s32[]{:S(2)}) async-start(), calls=%async_computation.4 | async-start | bytes 10485760 | tf_op jit(solution)/shard_map/all_gather | solution.py:172
  18.2 5.0 copy-start.60
  18.3 16.0 %copy-start.45 = (s32[32,4]{1,0:T(8,128)}, s32[32,4]{1,0:T(8,128)S(1)}, u32[]{:S(2)}) copy-start(s32[32,4]{1,0:T(8,128)S(1)} %copy.198) | copy-start | bytes 1540
  27.5 133.4 %copy-start.47 = (s32[1024]{0:T(1024)}, s32[1024]{0:T(1024)S(1)}, u32[]{:S(2)}) copy-start(s32[1024]{0:T(1024)S(1)} %fusion.96) | copy-start | bytes 12292
  34.4 82.3 %copy-start.64 = (s32[128]{0:T(128)}, s32[128]{0:T(128)S(1)}, u32[]{:S(2)}) copy-start(s32[128]{0:T(128)S(1)} %fusion.101) | copy-start | bytes 1540
  123.6 4.1 copy-start.11
  140.4 4.1 copy-start.11
  163.7 35.2 %copy-start.48 = (s32[1024]{0:T(1024)S(1)}, s32[1024]{0:T(1024)}, u32[]{:S(2)}) copy-start(s32[1024]{0:T(1024)} %copy-done.47) | copy-start | bytes 12292
  199.3 5.1 copy-start.46
  199.3 5.1 copy-start.57
  199.3 5.1 copy-start.59
  204.4 9.5 copy-start.19
  207.3 8.8 copy-start.25
  207.3 8.8 copy-start.31
  209.3 12.1 all-to-all-start
  221.4 6.5 copy-start.36
  221.4 9.6 all-to-all-start.2
  224.7 4.4 copy-start.65
  231.0 5.2 copy-start.40
  236.9 10.6 all-to-all-start.1
  247.4 9.6 all-to-all-start.3
  250.8 733.1 %all-reduce.11.cloned.1.call-start = ((), (), s32[]{:S(2)}) async-start(), calls=%async_computation.5 | async-start | bytes 8388608 | tf_op jit(solution)/shard_map/psum | solution.py:343
  270.2 3.9 copy-start.43
  270.2 3.9 copy-start.50
  270.3 3.9 copy-start.54
  274.2 4.9 copy-start.32
  289.0 4.6 copy-start.13
  289.0 4.6 copy-start.35
  299.0 7.9 copy-start.3
  299.0 7.9 copy-start.51
  308.5 8.5 copy-start.39
  317.1 9.3 copy-start.4
  341.4 6.1 copy-start.10
  350.3 8.5 copy-start.39
  358.9 9.3 copy-start.4
  383.2 6.1 copy-start.10
  401.9 497.4 %copy-start.16 = (bf16[1,1024,512]{1,2,0:T(8,128)(2,1)S(1)}, bf16[1,1024,512]{1,2,0:T(8,128)(2,1)}, u32[]{:S(2)}) copy-start(bf16[1,1024,512]{1,2,0:T(8,128)(2,1)} %copy-done.14) | copy-start | bytes 3145732
  401.9 497.4 %copy-start.56 = (f32[1024]{0:T(1024)S(1)}, f32[1024]{0:T(1024)}, u32[]{:S(2)}) copy-start(f32[1024]{0:T(1024)} %copy-done.55) | copy-start | bytes 12292
  401.9 497.4 %copy-start.62 = (f32[512]{0:T(512)S(1)}, f32[512]{0:T(512)}, u32[]{:S(2)}) copy-start(f32[512]{0:T(512)} %param.19) | copy-start | bytes 6148
  401.9 395.1 %collective-permute-start = (bf16[1024,1024]{1,0:T(8,128)(2,1)}, bf16[1024,1024]{1,0:T(8,128)(2,1)}, u32[]{:S(2)}, u32[]{:S(2)}) collective-permute-start(bf16[1024,1024]{1,0:T(8,128)(2,1)} %get-tuple-element.758), channel_id=1, source_target_pairs={{6,0},{0,2},{2,4},{4,6},{7,1},{1,3},{3,5},{5,7},{14,8},{8,10},{10,... | collective-permute-start | bytes 6291464 | tf_op jit(solution)/shard_map/while/body/eval_jaxpr/ppermute | solution.py:16
  802.0 44.1 %collective-permute-start = (bf16[1024,1024]{1,0:T(8,128)(2,1)}, bf16[1024,1024]{1,0:T(8,128)(2,1)}, u32[]{:S(2)}, u32[]{:S(2)}) collective-permute-start(bf16[1024,1024]{1,0:T(8,128)(2,1)} %get-tuple-element.758), channel_id=1, source_target_pairs={{6,0},{0,2},{2,4},{4,6},{7,1},{1,3},{3,5},{5,7},{14,8},{8,10},{10,... | collective-permute-start | bytes 6291464 | tf_op jit(solution)/shard_map/while/body/eval_jaxpr/ppermute | solution.py:16
  851.1 43.2 %collective-permute-start = (bf16[1024,1024]{1,0:T(8,128)(2,1)}, bf16[1024,1024]{1,0:T(8,128)(2,1)}, u32[]{:S(2)}, u32[]{:S(2)}) collective-permute-start(bf16[1024,1024]{1,0:T(8,128)(2,1)} %get-tuple-element.758), channel_id=1, source_target_pairs={{6,0},{0,2},{2,4},{4,6},{7,1},{1,3},{3,5},{5,7},{14,8},{8,10},{10,... | collective-permute-start | bytes 6291464 | tf_op jit(solution)/shard_map/while/body/eval_jaxpr/ppermute | solution.py:16
  904.7 5.5 copy-start.41
  904.7 212.1 %all-reduce.15.cloned.1.call-start = ((), (), s32[]{:S(2)}) async-start(), calls=%async_computation.7 | async-start | bytes 16777216 | tf_op jit(solution)/shard_map/psum | solution.py:349
  905.6 4.6 copy-start.23
  913.7 361.0 %all-reduce.13.cloned.1.call-start = ((), (), s32[]{:S(2)}) async-start(), calls=%async_computation.6 | async-start | bytes 8388608 | tf_op jit(solution)/shard_map/psum | solution.py:342
  986.2 4.0 copy-start.8
  1116.9 6.8 copy-start.26
  (36 other events, 82.5 us)
Sparse Core Ops, SparseCore 0:
  14.5 90.2 all-gather.1
  904.8 79.0 all-reduce.10
  989.2 127.5 all-reduce.14
  1119.1 155.5 all-reduce.12
